TPU v7x, 32 devices: a whole 2x2x4 slice. The times are simulated.
32 devices in a mesh: leaf: 8 (over z, y), blk: 4 (over x, core).
Axes of the slice: x: 2, y: 2, z: 4, core: 2. Of those that a mesh axis runs over, the one named last changes fastest.
Arguments:
- leaf_ops: float32 [8, 1024, 1024], P('leaf', 'blk'), may hold values from -1 to 9, as said below
- leaf_flux: float32 [8, 16, 1024], P('leaf', None, 'blk'), may hold values from -6 to 6
- boundary_data: float32 [8, 16, 1024], P('leaf', None, 'blk'), may hold values from -6 to 6
Outputs:
- top_flux: float32 [8, 16, 512], P('leaf', None, 'blk')
- leaf_values: float32 [8, 16, 1024], P('leaf', None, 'blk')
Inputs may be any that keep to these rules, and one draw needn't show every extreme that they name: `leaf_ops`: every leaf operator is symmetric positive definite.
All inputs are finite; a program needn't handle non-finite values.
Results may differ from a plain program's by a relative error of at most 0.0001.
Values sent between devices are 32-bit elements; how exact they have to be, the bound alone decides.
No kernel may reach another device: no remote copies, remote signals or barrier semaphores. Data moves between devices by JAX's collectives and lax.ppermute only.
A program may use at most 64 MiB of HBM per device.

v0:
```python
import jax
import jax.numpy as jnp
from jax import lax
from jax.sharding import PartitionSpec as P

LEVELS = 3
HIGHEST = lax.Precision.HIGHEST


def swapped(block, axis, distance):
    count = lax.axis_size(axis)
    route = []
    for low in range(count):
        high = low | 1 << distance
        if high != low and high < count:
            route += [(low, high), (high, low)]
    return lax.ppermute(block, axis, route)


def to_edge_major(values, quarter):
    leading = values.shape[:-1]
    grid = values.reshape(leading + (4, 4, quarter))
    return jnp.swapaxes(grid, -3, -2).reshape(leading + (16 * quarter,))


def halving_sum(payload, leaf_index, level_index):
    for bit_index in range(level_index + 1):
        half_rows = payload.shape[0] // 2
        is_upper = leaf_index // 2**bit_index % 2 == 1
        kept_half = jnp.where(is_upper, payload[half_rows:], payload[:half_rows])
        sent_half = jnp.where(is_upper, payload[:half_rows], payload[half_rows:])
        payload = kept_half + swapped(sent_half, "leaf", bit_index)
    for bit_index in reversed(range(level_index + 1)):
        is_upper = leaf_index // 2**bit_index % 2 == 1
        partner = swapped(payload, "leaf", bit_index)
        payload = jnp.where(
            is_upper,
            jnp.concatenate([partner, payload], axis=0),
            jnp.concatenate([payload, partner], axis=0),
        )
    return payload


def per_device(leaf_ops, leaf_flux, boundary_data):
    points = leaf_ops.shape[1]
    quarter = points // 4
    rhs_count = leaf_flux.shape[1]
    operator = to_edge_major(leaf_ops[0], quarter)
    fluxes = leaf_flux[0]
    leaf_index = lax.axis_index("leaf")
    saved = []
    for level_index in range(LEVELS):
        width = 2**level_index
        middle = 2 * points * width
        position = leaf_index % (2 * width)
        in_right = position >= width
        east_rows = operator[3 * quarter :]
        west_rows = operator[2 * quarter : 3 * quarter]
        blank_mid = jnp.zeros((quarter, middle), jnp.float32)
        blank_edge = jnp.zeros((quarter, points), jnp.float32)
        from_left = jnp.concatenate(
            [
                east_rows[:, middle + points :],
                east_rows[:, :middle],
                blank_mid,
                east_rows[:, middle : middle + points],
                blank_edge,
                fluxes[:, 3 * quarter :].T,
            ],
            axis=1,
        )
        from_right = jnp.concatenate(
            [
                west_rows[:, middle : middle + points],
                blank_mid,
                west_rows[:, :middle],
                blank_edge,
                west_rows[:, middle + points :],
                fluxes[:, 2 * quarter : 3 * quarter].T,
            ],
            axis=1,
        )
        payload = jnp.where(position == width - 1, from_left, 0.0) + jnp.where(
            position == width, from_right, 0.0
        )
        payload = halving_sum(payload, leaf_index, level_index)
        combined = lax.all_gather(payload, "blk", axis=0, tiled=True)
        parent_width = 2 * middle + 2 * points
        schur_block = combined[:, :points]
        coupling = combined[:, points : points + parent_width]
        flux_sum = combined[:, points + parent_width :]
        factor = jnp.linalg.cholesky(schur_block)
        offset = middle + points - points * in_right.astype(jnp.int32)
        shared = lax.dynamic_slice_in_dim(operator, offset, points, 1)
        solved = jax.scipy.linalg.cho_solve((factor, True), shared.T)
        blank_rows = jnp.zeros((points, middle), jnp.float32)
        blank_side = jnp.zeros((points, points), jnp.float32)
        left_ext = jnp.concatenate(
            [operator[:, :middle], blank_rows, operator[:, middle : middle + points], blank_side],
            axis=1,
        )
        right_ext = jnp.concatenate(
            [blank_rows, operator[:, :middle], blank_side, operator[:, middle + points :]], axis=1
        )
        operator = jnp.where(in_right, right_ext, left_ext) - jnp.dot(
            solved.T, coupling, precision=HIGHEST
        )
        fluxes = fluxes - jnp.dot(flux_sum.T, solved, precision=HIGHEST)
        saved.append((factor, coupling, flux_sum, in_right, middle))
    box_data = lax.all_gather(boundary_data[0], "blk", axis=1, tiled=True)
    box_data = to_edge_major(box_data, quarter)
    collected = box_data[:, None, :]
    for bit_index in range(LEVELS):
        partner = swapped(collected, "leaf", bit_index)
        is_upper = leaf_index // 2**bit_index % 2 == 1
        collected = jnp.where(
            is_upper,
            jnp.concatenate([partner, collected], axis=1),
            jnp.concatenate([collected, partner], axis=1),
        )
    count = 2**LEVELS
    potential = jnp.concatenate(
        [
            collected[:, :, : 2 * points].reshape(rhs_count, count * 2 * points),
            collected[:, 0, 2 * points : 3 * points],
            collected[:, count - 1, 3 * points :],
        ],
        axis=1,
    )
    outward = (
        jnp.dot(potential, operator[: 2 * quarter].T, precision=HIGHEST) + fluxes[:, : 2 * quarter]
    )
    for factor, coupling, flux_sum, in_right, middle in reversed(saved):
        inner = -jax.scipy.linalg.cho_solve(
            (factor, True), jnp.dot(coupling, potential.T, precision=HIGHEST) + flux_sum
        )
        left_part = jnp.concatenate(
            [potential[:, :middle], potential[:, 2 * middle : 2 * middle + points], inner.T], axis=1
        )
        right_part = jnp.concatenate(
            [potential[:, middle : 2 * middle], inner.T, potential[:, 2 * middle + points :]],
            axis=1,
        )
        potential = jnp.where(in_right, right_part, left_part)
    grid = potential.reshape(rhs_count, 4, 4, quarter)
    own_part = lax.dynamic_index_in_dim(grid, lax.axis_index("blk"), 2, keepdims=False).reshape(
        rhs_count, points
    )
    return (outward[None], own_part[None])


def solution(mesh):
    placed = (P("leaf", "blk", None), P("leaf", None, "blk"), P("leaf", None, "blk"))
    return jax.shard_map(
        per_device,
        mesh=mesh,
        in_specs=placed,
        out_specs=(P("leaf", None, "blk"), P("leaf", None, "blk")),
        check_vma=False,
    )
```

profile of v0, /device:TPU:0, one launch (start us, length us, event | category | flops | bytes accessed | tf_op | source)
XLA Modules:
  0.0 464.7 jit_solution(5282672462382747299)
XLA Ops:
  7.2 1.6 copy.133
  10.9 3.1 collective-permute-start.3
  14.0 6.0 %collective-permute-done.3 = f32[32,1808]{1,0:T(8,128)S(1)} collective-permute-done((f32[32,1808]{1,0:T(8,128)S(1)}, f32[32,1808]{1,0:T(8,128)S(1)}, u32[]{:S(2)}, u32[]{:S(2)}) %collective-permute-start.3) | collective-permute-done | bytes 231456 | tf_op jit(solution)/shard_map/ppermute | solution.py:17
  20.0 1.8 collective-permute-start.4
  21.8 5.4 %collective-permute-done.4 = f32[32,1808]{1,0:T(8,128)S(1)} collective-permute-done((f32[32,1808]{1,0:T(8,128)S(1)}, f32[32,1808]{1,0:T(8,128)S(1)}, u32[]{:S(2)}, u32[]{:S(2)}) %collective-permute-start.4) | collective-permute-done | bytes 231456 | tf_op jit(solution)/shard_map/ppermute | solution.py:17
  31.2 20.0 %all-gather.5.cloned.1.call-done = f32[256,1808]{1,0:T(8,128)} async-done(((f32[64,1808]{1,0:T(8,128)}), f32[256,1808]{1,0:T(8,128)}) %all-gather.5.cloned.1.call-update) | async-done | bytes 1851408 | tf_op jit(solution)/shard_map/all_gather | solution.py:87
  53.3 11.7 %cholesky.172 = f32[128,128]{1,0:T(8,128)S(1)} custom-call(f32[128,128]{1,0:T(8,128)S(1)} %cholesky.270), custom_call_target="Cholesky" | custom-call | tf_op jit(solution)/shard_map/jit(cholesky)/cholesky | solution.py:92
  65.1 9.8 %custom-call.24 = f32[1,128,128]{1,2,0:T(8,128)S(1)} custom-call(f32[1,128,128]{2,1,0:T(8,128)S(1)} %get-tuple-element.137), custom_call_target="InvertDiagBlocksLowerTriangular" | custom-call | tf_op jit(solution)/shard_map/jit(cholesky)/cholesky | solution.py:92
  75.4 11.7 %cholesky.189 = f32[128,128]{1,0:T(8,128)S(1)} custom-call(f32[128,128]{1,0:T(8,128)S(1)} %convolution_subtract_fusion.12), custom_call_target="Cholesky" | custom-call | tf_op jit(solution)/shard_map/jit(cholesky)/cholesky | solution.py:92
  89.8 4.1 while.12
  93.9 19.7 %custom-call.25 = f32[2,128,128]{1,2,0:T(8,128)S(1)} custom-call(f32[2,128,128]{2,1,0:T(8,128)S(1)} %get-tuple-element.45), custom_call_target="InvertDiagBlocksLowerTriangular" | custom-call | tf_op jit(solution)/shard_map/jit(_cho_solve)/triangular_solve | solution.py:95
  116.1 3.4 convolution_subtract_fusion.1
  123.3 9.4 %collective-permute-done.5 = f32[32,2832]{1,0:T(8,128)S(1)} collective-permute-done((f32[32,2832]{1,0:T(8,128)S(1)}, f32[32,2832]{1,0:T(8,128)S(1)}, u32[]{:S(2)}, u32[]{:S(2)}) %collective-permute-start.5) | collective-permute-done | bytes 362528 | tf_op jit(solution)/shard_map/ppermute | solution.py:17
  132.9 1.6 collective-permute-start.6
  134.4 4.5 collective-permute-done.6
  139.0 1.6 collective-permute-start.7
  140.5 4.1 collective-permute-done.7
  146.2 6.6 %collective-permute-done.8 = f32[32,2832]{1,0:T(8,128)S(1)} collective-permute-done((f32[32,2832]{1,0:T(8,128)S(1)}, f32[32,2832]{1,0:T(8,128)S(1)}, u32[]{:S(2)}, u32[]{:S(2)}) %collective-permute-start.8) | collective-permute-done | bytes 362528 | tf_op jit(solution)/shard_map/ppermute | solution.py:17
  156.2 25.4 %all-gather.7.cloned.1.call-done = f32[256,2832]{1,0:T(8,128)} async-done(((f32[64,2832]{1,0:T(8,128)}), f32[256,2832]{1,0:T(8,128)}) %all-gather.7.cloned.1.call-update) | async-done | bytes 2899984 | tf_op jit(solution)/shard_map/all_gather | solution.py:87
  183.7 11.7 %cholesky.206 = f32[128,128]{1,0:T(8,128)S(1)} custom-call(f32[128,128]{1,0:T(8,128)S(1)} %cholesky.273), custom_call_target="Cholesky" | custom-call | tf_op jit(solution)/shard_map/jit(cholesky)/cholesky | solution.py:92
  195.5 9.8 %custom-call.26 = f32[1,128,128]{1,2,0:T(8,128)S(1)} custom-call(f32[1,128,128]{2,1,0:T(8,128)S(1)} %get-tuple-element.133), custom_call_target="InvertDiagBlocksLowerTriangular" | custom-call | tf_op jit(solution)/shard_map/jit(cholesky)/cholesky | solution.py:92
  205.8 11.7 %cholesky.223 = f32[128,128]{1,0:T(8,128)S(1)} custom-call(f32[128,128]{1,0:T(8,128)S(1)} %convolution_subtract_fusion.11), custom_call_target="Cholesky" | custom-call | tf_op jit(solution)/shard_map/jit(cholesky)/cholesky | solution.py:92
  220.4 4.4 while.13
  224.8 19.7 %custom-call.27 = f32[2,128,128]{1,2,0:T(8,128)S(1)} custom-call(f32[2,128,128]{2,1,0:T(8,128)S(1)} %get-tuple-element.46), custom_call_target="InvertDiagBlocksLowerTriangular" | custom-call | tf_op jit(solution)/shard_map/jit(_cho_solve)/triangular_solve | solution.py:95
  246.5 5.6 %convolution_subtract_fusion = f32[256,2560]{1,0:T(8,128)S(1)} fusion(f32[256,256]{1,0:T(8,128)} %get-tuple-element.96, f32[256,256]{1,0:T(8,128)} %copy-done.19, f32[256,1024]{1,0:T(8,128)} %slice.436, f32[256,1024]{1,0:T(8,128)S(1)} %broadcast_in_dim.38, f32[256,256]{1,0:T(8,128)} %get-tuple-element.95, f32[256,2832]{1,0:T(8,128)} %all-gather.7.cloned.1.call-done, ...), kind=kOutput, calls=%fused_computation.10 | convolution fusion | flops 2018574336 | bytes 8388609 | tf_op jit(solution)/shard_map/dot_general | solution.py:105
  252.4 2.5 copy-done.1
  258.0 15.0 %collective-permute-done.9 = f32[32,4880]{1,0:T(8,128)S(1)} collective-permute-done((f32[32,4880]{1,0:T(8,128)S(1)}, f32[32,4880]{1,0:T(8,128)S(1)}, u32[]{:S(2)}, u32[]{:S(2)}) %collective-permute-start.9) | collective-permute-done | bytes 624672 | tf_op jit(solution)/shard_map/ppermute | solution.py:17
  275.3 7.6 %collective-permute-done.10 = f32[16,4880]{1,0:T(8,128)} collective-permute-done((f32[16,4880]{1,0:T(8,128)}, f32[16,4880]{1,0:T(8,128)}, u32[]{:S(2)}, u32[]{:S(2)}) %collective-permute-start.10) | collective-permute-done | bytes 312352 | tf_op jit(solution)/shard_map/ppermute | solution.py:17
  284.0 2.5 collective-permute-start.11
  286.5 6.4 %collective-permute-done.11 = f32[8,4880]{1,0:T(8,128)S(1)} collective-permute-done((f32[8,4880]{1,0:T(8,128)S(1)}, f32[8,4880]{1,0:T(8,128)S(1)}, u32[]{:S(2)}, u32[]{:S(2)}) %collective-permute-start.11) | collective-permute-done | bytes 156192 | tf_op jit(solution)/shard_map/ppermute | solution.py:17
  293.1 9.4 %collective-permute-done.12 = f32[8,4880]{1,0:T(8,128)S(1)} collective-permute-done((f32[8,4880]{1,0:T(8,128)S(1)}, f32[8,4880]{1,0:T(8,128)S(1)}, u32[]{:S(2)}, u32[]{:S(2)}) %collective-permute-start.12) | collective-permute-done | bytes 156192 | tf_op jit(solution)/shard_map/ppermute | solution.py:17
  302.6 8.5 %collective-permute-done.13 = f32[16,4880]{1,0:T(8,128)S(1)} collective-permute-done((f32[16,4880]{1,0:T(8,128)S(1)}, f32[16,4880]{1,0:T(8,128)S(1)}, u32[]{:S(2)}, u32[]{:S(2)}) %collective-permute-start.13) | collective-permute-done | bytes 312352 | tf_op jit(solution)/shard_map/ppermute | solution.py:17
  311.2 1.5 collective-permute-start.14
  312.7 13.0 %collective-permute-done.14 = f32[32,4880]{1,0:T(8,128)S(1)} collective-permute-done((f32[32,4880]{1,0:T(8,128)S(1)}, f32[32,4880]{1,0:T(8,128)S(1)}, u32[]{:S(2)}, u32[]{:S(2)}) %collective-permute-start.14) | collective-permute-done | bytes 624672 | tf_op jit(solution)/shard_map/ppermute | solution.py:17
  326.9 5.4 %all-gather = f32[1,16,1024]{2,1,0:T(8,128)S(1)} all-gather(f32[1,16,256]{2,1,0:T(8,128)S(1)} %copy-done.24), channel_id=2, replica_groups=mesh['leaf'=8,'blk'=4] {'blk'}, dimensions={2}, use_global_device_ids=true | all-gather | bytes 81920 | tf_op jit(solution)/shard_map/all_gather | solution.py:110
  334.2 2.9 collective-permute-done
  337.7 4.4 collective-permute-done.1
  343.4 12.4 %collective-permute-done.2 = f32[16,4,1024]{2,0,1:T(8,128)} collective-permute-done((f32[16,4,1024]{2,0,1:T(8,128)S(1)}, f32[16,4,1024]{2,0,1:T(8,128)}, u32[]{:S(2)}, u32[]{:S(2)}) %collective-permute-start.2) | collective-permute-done | bytes 262176 | tf_op jit(solution)/shard_map/ppermute | solution.py:17
  359.6 6.1 %all-gather.9.cloned.1.call-done = f32[256,4880]{1,0:T(8,128)} async-done(((f32[64,4880]{1,0:T(8,128)}), f32[256,4880]{1,0:T(8,128)}) %all-gather.9.cloned.1.call-update) | async-done | bytes 4997136 | tf_op jit(solution)/shard_map/all_gather | solution.py:87
  368.8 11.7 %cholesky.240 = f32[128,128]{1,0:T(8,128)S(1)} custom-call(f32[128,128]{1,0:T(8,128)S(1)} %cholesky.276), custom_call_target="Cholesky" | custom-call | tf_op jit(solution)/shard_map/jit(cholesky)/cholesky | solution.py:92
  380.6 9.8 %custom-call.28 = f32[1,128,128]{1,2,0:T(8,128)S(1)} custom-call(f32[1,128,128]{2,1,0:T(8,128)S(1)} %get-tuple-element.129), custom_call_target="InvertDiagBlocksLowerTriangular" | custom-call | tf_op jit(solution)/shard_map/jit(cholesky)/cholesky | solution.py:92
  390.9 11.7 %cholesky.257 = f32[128,128]{1,0:T(8,128)S(1)} custom-call(f32[128,128]{1,0:T(8,128)S(1)} %convolution_subtract_fusion.10), custom_call_target="Cholesky" | custom-call | tf_op jit(solution)/shard_map/jit(cholesky)/cholesky | solution.py:92
  405.1 4.2 while.14
  409.4 19.7 %custom-call.29 = f32[2,128,128]{1,2,0:T(8,128)S(1)} custom-call(f32[2,128,128]{2,1,0:T(8,128)S(1)} %get-tuple-element.47), custom_call_target="InvertDiagBlocksLowerTriangular" | custom-call | tf_op jit(solution)/shard_map/jit(_cho_solve)/triangular_solve | solution.py:95
  429.1 6.2 %fusion.24 = f32[256,16]{0,1:T(8,128)S(1)} fusion(f32[256,16]{0,1:T(8,128)S(1)} %copy.171, f32[256,4880]{1,0:T(8,128)} %all-gather.9.cloned.1.call-done, f32[16,256]{1,0:T(8,128)S(1)} %get-tuple-element.109, f32[16,256]{1,0:T(8,128)S(1)} %get-tuple-element.108, f32[16,4096]{1,0:T(8,128)S(1)} %bitcast.210), kind=kOutput, calls=%fused_computation.49 | convolution fusion | flops 226643968 | bytes 5046272 | tf_op jit(solution)/shard_map/dot_general | solution.py:135
  436.6 2.1 fusion.21
  447.0 6.4 %fusion.2 = f32[256,4608]{1,0:T(8,128)S(1)} fusion(f32[256,4880]{1,0:T(8,128)} %all-gather.9.cloned.1.call-done, f32[128,256]{1,0:T(8,128)S(1)} %fusion.65, f32[128,256]{1,0:T(8,128)S(1)} %fusion.62), kind=kOutput, calls=%fused_computation.8 | convolution fusion | flops 3623944192 | bytes 9699328 | tf_op jit(solution)/shard_map/dot_general | solution.py:105
  454.9 2.0 fusion.17
  (267 shorter events, 71.2 us)
Async XLA Ops:
  7.2 44.0 %all-gather.5.cloned.1.call-start = ((), (), s32[]{:S(2)}) async-start(), calls=%async_computation | async-start | bytes 2457600 | tf_op jit(solution)/shard_map/all_gather | solution.py:87
  9.3 1.3 copy-start.23
  10.8 17.2 %copy-start.13 = (f32[1,16,256]{1,2,0:T(8,128)}, f32[1,16,256]{1,2,0:T(8,128)S(1)}, u32[]{:S(2)}) copy-start(f32[1,16,256]{1,2,0:T(8,128)S(1)} %copy.139) | copy-start | bytes 49156
  10.9 9.0 %collective-permute-start.3 = (f32[32,1808]{1,0:T(8,128)S(1)}, f32[32,1808]{1,0:T(8,128)S(1)}, u32[]{:S(2)}, u32[]{:S(2)}) collective-permute-start(f32[32,1808]{1,0:T(8,128)S(1)} %slice_select_fusion.3), channel_id=1, source_target_pairs={{0,4},{4,0},{8,12},{12,8},{16,20},{20,16},{24,28},{28,24},{1,5},{5... | collective-permute-start | bytes 694280 | tf_op jit(solution)/shard_map/ppermute | solution.py:17
  20.0 7.2 %collective-permute-start.4 = (f32[32,1808]{1,0:T(8,128)S(1)}, f32[32,1808]{1,0:T(8,128)S(1)}, u32[]{:S(2)}, u32[]{:S(2)}) collective-permute-start(f32[32,1808]{1,0:T(8,128)S(1)} %select_add_fusion.6), channel_id=1, source_target_pairs={{0,4},{4,0},{8,12},{12,8},{16,20},{20,16},{24,28},{28,24},{1,5},{5... | collective-permute-start | bytes 694280 | tf_op jit(solution)/shard_map/ppermute | solution.py:17
  28.0 153.6 %all-gather.7.cloned.1.call-start = ((), (), s32[]{:S(2)}) async-start(), calls=%async_computation.1 | async-start | bytes 3768320 | tf_op jit(solution)/shard_map/all_gather | solution.py:87
  113.5 5.9 %copy-start.7 = (f32[2,128,128]{1,2,0:T(8,128)}, f32[2,128,128]{1,2,0:T(8,128)S(1)}, u32[]{:S(2)}) copy-start(f32[2,128,128]{1,2,0:T(8,128)S(1)} %custom-call.25) | copy-start | bytes 393220
  115.3 0.7 copy-start.19
  119.5 1.5 copy-start.3
  119.5 1.5 copy-start.14
  121.6 11.2 %copy-start.11 = (f32[16,256]{0,1:T(8,128)}, f32[16,256]{0,1:T(8,128)S(1)}, u32[]{:S(2)}) copy-start(f32[16,256]{0,1:T(8,128)S(1)} %convolution_subtract_fusion.3) | copy-start | bytes 49156
  121.8 11.0 %collective-permute-start.5 = (f32[32,2832]{1,0:T(8,128)S(1)}, f32[32,2832]{1,0:T(8,128)S(1)}, u32[]{:S(2)}, u32[]{:S(2)}) collective-permute-start(f32[32,2832]{1,0:T(8,128)S(1)} %slice_select_fusion.1), channel_id=1, source_target_pairs={{0,4},{4,0},{8,12},{12,8},{16,20},{20,16},{24,28},{28,24},{1,5},{5... | collective-permute-start | bytes 1087496 | tf_op jit(solution)/shard_map/ppermute | solution.py:17
  132.9 6.1 %collective-permute-start.6 = (f32[16,2832]{1,0:T(8,128)S(1)}, f32[16,2832]{1,0:T(8,128)S(1)}, u32[]{:S(2)}, u32[]{:S(2)}) collective-permute-start(f32[16,2832]{1,0:T(8,128)S(1)} %slice_select_fusion.4), channel_id=1, source_target_pairs={{0,8},{8,0},{4,12},{12,4},{16,24},{24,16},{20,28},{28,20},{1,9},{9... | collective-permute-start | bytes 543752 | tf_op jit(solution)/shard_map/ppermute | solution.py:17
  139.0 5.6 %collective-permute-start.7 = (f32[16,2832]{1,0:T(8,128)S(1)}, f32[16,2832]{1,0:T(8,128)S(1)}, u32[]{:S(2)}, u32[]{:S(2)}) collective-permute-start(f32[16,2832]{1,0:T(8,128)S(1)} %select_add_fusion.7), channel_id=1, source_target_pairs={{0,8},{8,0},{4,12},{12,4},{16,24},{24,16},{20,28},{28,20},{1,9},{9... | collective-permute-start | bytes 543752 | tf_op jit(solution)/shard_map/ppermute | solution.py:17
  144.7 8.1 %collective-permute-start.8 = (f32[32,2832]{1,0:T(8,128)S(1)}, f32[32,2832]{1,0:T(8,128)S(1)}, u32[]{:S(2)}, u32[]{:S(2)}) collective-permute-start(f32[32,2832]{1,0:T(8,128)S(1)} %maximum_select_fusion.7), channel_id=1, source_target_pairs={{0,4},{4,0},{8,12},{12,8},{16,20},{20,16},{24,28},{28,24},{1,5},{5... | collective-permute-start | bytes 1087496 | tf_op jit(solution)/shard_map/ppermute | solution.py:17
  153.7 212.0 %all-gather.9.cloned.1.call-start = ((), (), s32[]{:S(2)}) async-start(), calls=%async_computation.2 | async-start | bytes 6389760 | tf_op jit(solution)/shard_map/all_gather | solution.py:87
  224.7 21.6 %copy-start.5 = (f32[256,256]{1,0:T(8,128)}, f32[256,256]{1,0:T(8,128)S(1)}, u32[]{:S(2)}) copy-start(f32[256,256]{1,0:T(8,128)S(1)} %get-tuple-element.289) | copy-start | bytes 786436
  224.8 27.4 %copy-start.25 = (s32[2,2]{1,0:T(2,128)}, s32[2,2]{1,0:T(2,128)S(1)}, u32[]{:S(2)}) copy-start(s32[2,2]{1,0:T(2,128)S(1)} %get-tuple-element.321) | copy-start | bytes 52
  244.5 1.9 copy-start.9
  252.1 106.6 %copy-start = (f32[256,2560]{1,0:T(8,128)}, f32[256,2560]{1,0:T(8,128)S(1)}, u32[]{:S(2)}) copy-start(f32[256,2560]{1,0:T(8,128)S(1)} %convolution_subtract_fusion) | copy-start | bytes 7864324
  252.2 2.8 copy-start.1
  252.2 2.8 copy-start.12
  255.6 0.7 copy-start.17
  256.4 16.6 %collective-permute-start.9 = (f32[32,4880]{1,0:T(8,128)S(1)}, f32[32,4880]{1,0:T(8,128)S(1)}, u32[]{:S(2)}, u32[]{:S(2)}) collective-permute-start(f32[32,4880]{1,0:T(8,128)S(1)} %slice_select_fusion), channel_id=1, source_target_pairs={{0,4},{4,0},{8,12},{12,8},{16,20},{20,16},{24,28},{28,24},{1,5},{5... | collective-permute-start | bytes 1873928 | tf_op jit(solution)/shard_map/ppermute | solution.py:17
  273.9 9.1 %collective-permute-start.10 = (f32[16,4880]{1,0:T(8,128)}, f32[16,4880]{1,0:T(8,128)}, u32[]{:S(2)}, u32[]{:S(2)}) collective-permute-start(f32[16,4880]{1,0:T(8,128)} %slice_select_fusion.2), channel_id=1, source_target_pairs={{0,8},{8,0},{4,12},{12,4},{16,24},{24,16},{20,28},{28,20},{1,9},{9... | collective-permute-start | bytes 936968 | tf_op jit(solution)/shard_map/ppermute | solution.py:17
  284.0 8.9 %collective-permute-start.11 = (f32[8,4880]{1,0:T(8,128)S(1)}, f32[8,4880]{1,0:T(8,128)S(1)}, u32[]{:S(2)}, u32[]{:S(2)}) collective-permute-start(f32[8,4880]{1,0:T(8,128)S(1)} %slice_select_fusion.5), channel_id=1, source_target_pairs={{0,16},{16,0},{4,20},{20,4},{8,24},{24,8},{12,28},{28,12},{1,17},{... | collective-permute-start | bytes 468488 | tf_op jit(solution)/shard_map/ppermute | solution.py:17
  293.0 9.5 %collective-permute-start.12 = (f32[8,4880]{1,0:T(8,128)S(1)}, f32[8,4880]{1,0:T(8,128)S(1)}, u32[]{:S(2)}, u32[]{:S(2)}) collective-permute-start(f32[8,4880]{1,0:T(8,128)S(1)} %select_add_fusion.8), channel_id=1, source_target_pairs={{0,16},{16,0},{4,20},{20,4},{8,24},{24,8},{12,28},{28,12},{1,17},{... | collective-permute-start | bytes 468488 | tf_op jit(solution)/shard_map/ppermute | solution.py:17
  302.5 8.6 %collective-permute-start.13 = (f32[16,4880]{1,0:T(8,128)S(1)}, f32[16,4880]{1,0:T(8,128)S(1)}, u32[]{:S(2)}, u32[]{:S(2)}) collective-permute-start(f32[16,4880]{1,0:T(8,128)S(1)} %maximum_select_fusion.8), channel_id=1, source_target_pairs={{0,8},{8,0},{4,12},{12,4},{16,24},{24,16},{20,28},{28,20},{1,9},{9... | collective-permute-start | bytes 936968 | tf_op jit(solution)/shard_map/ppermute | solution.py:17
  311.2 15.7 %copy-start.24 = (f32[1,16,256]{2,1,0:T(8,128)S(1)}, f32[1,16,256]{2,1,0:T(8,128)}, u32[]{:S(2)}) copy-start(f32[1,16,256]{2,1,0:T(8,128)} %param.10) | copy-start | bytes 49156
  311.2 14.6 %collective-permute-start.14 = (f32[32,4880]{1,0:T(8,128)S(1)}, f32[32,4880]{1,0:T(8,128)S(1)}, u32[]{:S(2)}, u32[]{:S(2)}) collective-permute-start(f32[32,4880]{1,0:T(8,128)S(1)} %maximum_select_fusion.4), channel_id=1, source_target_pairs={{0,4},{4,0},{8,12},{12,8},{16,20},{20,16},{24,28},{28,24},{1,5},{5... | collective-permute-start | bytes 1873928 | tf_op jit(solution)/shard_map/ppermute | solution.py:17
  332.5 25.1 %slice-start.2 = ((f32[256,1808]{1,0:T(8,128)}), f32[256,16]{1,0:T(8,128)S(1)}, s32[]{:S(2)}) async-start(f32[256,1808]{1,0:T(8,128)} %all-gather.5.cloned.1.call-done), calls=%async_computation.5 | async-start | bytes 262144
  332.7 4.4 collective-permute-start
  337.1 5.0 %collective-permute-start.1 = (f32[16,2,1024]{2,0,1:T(8,128)S(1)}, f32[16,2,1024]{2,0,1:T(8,128)S(1)}, u32[]{:S(2)}, u32[]{:S(2)}) collective-permute-start(f32[16,2,1024]{2,0,1:T(8,128)S(1)} %maximum_select_fusion.11), channel_id=1, source_target_pairs={{0,8},{8,0},{4,12},{12,4},{16,24},{24,16},{20,28},{28,20},{1,9},{9... | collective-permute-start | bytes 393224 | tf_op jit(solution)/shard_map/ppermute | solution.py:17
  342.2 13.6 %collective-permute-start.2 = (f32[16,4,1024]{2,0,1:T(8,128)S(1)}, f32[16,4,1024]{2,0,1:T(8,128)}, u32[]{:S(2)}, u32[]{:S(2)}) collective-permute-start(f32[16,4,1024]{2,0,1:T(8,128)S(1)} %maximum_select_fusion.9), channel_id=1, source_target_pairs={{0,16},{16,0},{4,20},{20,4},{8,24},{24,8},{12,28},{28,12},{1,17},{... | collective-permute-start | bytes 786440 | tf_op jit(solution)/shard_map/ppermute | solution.py:17
  357.7 0.9 slice-start.1
  366.6 38.5 %copy-start.26 = (s32[2,2]{1,0:T(2,128)S(1)}, s32[2,2]{1,0:T(2,128)}, u32[]{:S(2)}) copy-start(s32[2,2]{1,0:T(2,128)} %copy-done.25) | copy-start | bytes 52
  429.1 7.5 %copy-start.15 = (f32[16,2048]{1,0:T(8,128)S(1)}, f32[16,2048]{1,0:T(8,128)}, u32[]{:S(2)}) copy-start(f32[16,2048]{1,0:T(8,128)} %get-tuple-element.110) | copy-start | bytes 393220
  429.1 7.5 %copy-start.16 = (f32[16,2048]{1,0:T(8,128)S(1)}, f32[16,2048]{1,0:T(8,128)}, u32[]{:S(2)}) copy-start(f32[16,2048]{1,0:T(8,128)} %get-tuple-element.111) | copy-start | bytes 393220
  429.1 7.5 %copy-start.2 = (f32[256,2832]{1,0:T(8,128)S(1)}, f32[256,2832]{1,0:T(8,128)}, u32[]{:S(2)}) copy-start(f32[256,2832]{1,0:T(8,128)} %all-gather.7.cloned.1.call-done) | copy-start | bytes 8699908
  435.9 2.9 copy-start.10
  436.1 2.9 copy-start.6
  436.6 3.4 copy-start.4
  438.8 2.6 copy-start.8
  446.9 6.7 %copy-start.18 = (f32[16,256]{0,1:T(8,128)S(1)}, f32[16,256]{0,1:T(8,128)}, u32[]{:S(2)}) copy-start(f32[16,256]{0,1:T(8,128)} %copy-done.17) | copy-start | bytes 49156
  446.9 6.7 %copy-start.20 = (f32[256,256]{1,0:T(8,128)S(1)}, f32[256,256]{1,0:T(8,128)}, u32[]{:S(2)}) copy-start(f32[256,256]{1,0:T(8,128)} %copy-done.19) | copy-start | bytes 786436
  446.9 6.7 %copy-start.21 = (f32[256,256]{1,0:T(8,128)S(1)}, f32[256,256]{1,0:T(8,128)}, u32[]{:S(2)}) copy-start(f32[256,256]{1,0:T(8,128)} %get-tuple-element.85) | copy-start | bytes 786436
  446.9 6.7 %copy-start.22 = (f32[256,256]{1,0:T(8,128)S(1)}, f32[256,256]{1,0:T(8,128)}, u32[]{:S(2)}) copy-start(f32[256,256]{1,0:T(8,128)} %get-tuple-element.87) | copy-start | bytes 786436
  453.3 1.6 slice-start
Sparse Core Ops, SparseCore 0:
  28.1 23.0 all-gather.4
  153.8 27.7 all-gather.6
  327.0 38.5 all-gather.8
where the time goes:
time: 468 us; the launch traced here: 465 us
  other arithmetic  173 us (37%)
  waiting for transfers between devices  167 us (36%)
  matrix products  40 us (9%)
  local copies, waits for them, and re-layouts  36.5 us (8%)
  starting transfers between devices  22.5 us (5%)
  between operations  19.4 us (4%)
  blocking collectives  5.45 us (1%)
    ppermute x15, waiting for transfers between devices, swapped(): return lax.ppermute(block, axis, route)  116 us
    another operation x21, other arithmetic, per_device(): factor = jnp.linalg.cholesky(schur_block)  104 us
    another operation x7, other arithmetic, per_device(): solved = jax.scipy.linalg.cho_solve((factor, True), shared.T)  59.1 us
    all_gather x3, waiting for transfers between devices, per_device(): combined = lax.all_gather(payload, 'blk', axis=0, tiled=True)  51.5 us
    ppermute x15, starting transfers between devices, swapped(): return lax.ppermute(block, axis, route)  21.7 us
    dot_general x3, matrix products, per_device(): jnp.dot(solved.T, coupling, precision=HIGHEST)  15.4 us
    unnamed x95, local copies, waits for them, and re-layouts  13.1 us
    another operation x22, local copies, waits for them, and re-layouts, per_device(): solved = jax.scipy.linalg.cho_solve((factor, True), shared.T)  12 us
  transfers between devices with their start and end apart: 18, of which 18 were waited for; matrix products, arithmetic and copies ran while one was open for 2% of the time, Pallas kernels for 0%

commit v1 on v0

--- a/solution.py
+++ b/solution.py
@@ -84,7 +84,14 @@
             position == width, from_right, 0.0
         )
         payload = halving_sum(payload, leaf_index, level_index)
-        combined = lax.all_gather(payload, "blk", axis=0, tiled=True)
+        ring = [payload]
+        for hop in range(3):
+            ring.append(lax.ppermute(ring[-1], "blk", [(dev, (dev + 1) % 4) for dev in range(4)]))
+        combined = jnp.roll(
+            jnp.concatenate(ring[::-1], axis=0),
+            (lax.axis_index("blk") + 1) * ring[0].shape[0],
+            axis=0,
+        )
         parent_width = 2 * middle + 2 * points
         schur_block = combined[:, :points]
         coupling = combined[:, points : points + parent_width]

time: 468 us -> 597 us (1.28)
  local copies, waits for them, and re-layouts: 36.5 us -> 126 us
  other arithmetic: 173 us -> 205 us
  between operations: 19.4 us -> 6.51 us
  blocking collectives: 5.45 us -> 17.7 us
  matrix products: 40 us -> 47.3 us
    ppermute x0 -> x9, waiting for transfers between devices: none -> 66.2 us  [per_device(): lax.ppermute(ring[-1], 'blk', [(dev, (dev + 1) % 4) for dev in range(4)])]
    all_gather x3 -> x0, waiting for transfers between devices: 51.5 us -> none  [per_device(): combined = lax.all_gather(payload, 'blk', axis=0, tiled=True)]
    ppermute x0 -> x19, local copies, waits for them, and re-layouts: none -> 40.4 us  [the longest x9 20.8 us: per_device(): lax.ppermute(ring[-1], 'blk', [(dev, (dev + 1) % 4) for dev in range(4)])]
    concatenate x0 -> x5, local copies, waits for them, and re-layouts: none -> 34.6 us  [the longest x3 30.1 us: per_device(): jnp.roll(jnp.concatenate(ring[::-1], axis=0), (lax.axis_index('blk') + 1)...]
    ppermute x15, waiting for transfers between devices: 116 us -> 97.6 us  [swapped(): return lax.ppermute(block, axis, route)]
    select_n x0 -> x11, local copies, waits for them, and re-layouts: none -> 14.9 us  [the longest x6 9.14 us: halving_sum(): sent_half = jnp.where(is_upper, payload[:half_rows], payload[half_rows:])]
    add x6, other arithmetic: 1.29 us -> 15.3 us  [halving_sum(): payload = kept_half + swapped(sent_half, 'leaf', bit_index)]
    all_gather x1, blocking collectives: 5.45 us -> 17.7 us  [per_device(): box_data = lax.all_gather(boundary_data[0], 'blk', axis=1, tiled=True)]
  transfers between devices with their start and end apart: 18 -> 24, of which waited for: 18 -> 22; matrix products, arithmetic and copies ran while one was open for 2% -> 3% of each run, Pallas kernels for 0% -> 0%
where the time goes in v1:
time: 597 us; the launch traced here: 592 us
  other arithmetic  205 us (34%)
  waiting for transfers between devices  164 us (27%)
  local copies, waits for them, and re-layouts  126 us (21%)
  matrix products  47.3 us (8%)
  starting transfers between devices  25.4 us (4%)
  blocking collectives  17.7 us (3%)
  between operations  6.51 us (1%)
    another operation x21, other arithmetic, per_device(): factor = jnp.linalg.cholesky(schur_block)  104 us
    ppermute x15, waiting for transfers between devices, swapped(): return lax.ppermute(block, axis, route)  97.6 us
    ppermute x9, waiting for transfers between devices, per_device(): lax.ppermute(ring[-1], 'blk', [(dev, (dev + 1) % 4) for dev in range(4)])  66.2 us
    another operation x7, other arithmetic, per_device(): solved = jax.scipy.linalg.cho_solve((factor, True), shared.T)  60.2 us
    concatenate x3, local copies, waits for them, and re-layouts, per_device(): jnp.roll(jnp.concatenate(ring[::-1], axis=0), (lax.axis_index('blk') + 1)...  30.1 us
    ppermute x15, starting transfers between devices, swapped(): return lax.ppermute(block, axis, route)  24.7 us
    ppermute x9, local copies, waits for them, and re-layouts, per_device(): lax.ppermute(ring[-1], 'blk', [(dev, (dev + 1) % 4) for dev in range(4)])  20.8 us
    ppermute x10, local copies, waits for them, and re-layouts, swapped(): return lax.ppermute(block, axis, route)  19.6 us
  transfers between devices with their start and end apart: 24, of which 22 were waited for; matrix products, arithmetic and copies ran while one was open for 3% of the time, Pallas kernels for 0%

profile of v1, /device:TPU:0, one launch (start us, length us, event | category | flops | bytes accessed | tf_op | source)
XLA Modules:
  0.0 591.9 jit_solution(148688026399838019)
XLA Ops:
  7.0 6.0 %collective-permute-done.3 = f32[32,1808]{1,0:T(8,128)S(1)} collective-permute-done((f32[32,1808]{1,0:T(8,128)S(1)}, f32[32,1808]{1,0:T(8,128)S(1)}, u32[]{:S(2)}, u32[]{:S(2)}) %collective-permute-start.3) | collective-permute-done | bytes 231456 | tf_op jit(solution)/shard_map/ppermute | solution.py:17
  17.8 5.4 collective-permute-done.4
  26.9 8.2 %collective-permute-done.5 = f32[64,1808]{1,0:T(8,128)S(1)} collective-permute-done((f32[64,1808]{1,0:T(8,128)S(1)}, f32[64,1808]{1,0:T(8,128)S(1)}, u32[]{:S(2)}, u32[]{:S(2)}) %collective-permute-start.5) | collective-permute-done | bytes 462880 | tf_op jit(solution)/shard_map/ppermute | solution.py:89
  35.9 8.4 %collective-permute-done.6 = f32[64,1808]{1,0:T(8,128)} collective-permute-done((f32[64,1808]{1,0:T(8,128)S(1)}, f32[64,1808]{1,0:T(8,128)}, u32[]{:S(2)}, u32[]{:S(2)}) %collective-permute-start.6) | collective-permute-done | bytes 462880 | tf_op jit(solution)/shard_map/ppermute | solution.py:89
  49.1 4.0 collective-permute-done.7
  55.4 6.1 %concatenate.150 = f32[512,1808]{0,1:T(8,128)} concatenate(f32[64,1808]{0,1:T(8,128)} %copy.171, f32[64,1808]{0,1:T(8,128)S(1)} %copy.172, f32[64,1808]{0,1:T(8,128)S(1)} %copy.173, f32[64,1808]{0,1:T(8,128)S(1)} %maximum_select_fusion.5, f32[64,1808]{0,1:T(8,128)} %copy.171, f32[64,1808]{0,1:T(8,128)S(1)} %copy.172, f32[64,1808]{0,1:T(8,128)S(1)} %copy.173, ...), dimensions={0} | concatenate | bytes 7405568 | tf_op jit(solution)/shard_map/jit(_roll_dynamic)/concatenate | solution.py:90
  63.9 11.7 %cholesky.172 = f32[128,128]{1,0:T(8,128)S(1)} custom-call(f32[128,128]{1,0:T(8,128)S(1)} %cholesky.270), custom_call_target="Cholesky" | custom-call | tf_op jit(solution)/shard_map/jit(cholesky)/cholesky | solution.py:99
  75.7 9.8 %custom-call.24 = f32[1,128,128]{1,2,0:T(8,128)S(1)} custom-call(f32[1,128,128]{2,1,0:T(8,128)S(1)} %get-tuple-element.129), custom_call_target="InvertDiagBlocksLowerTriangular" | custom-call | tf_op jit(solution)/shard_map/jit(cholesky)/cholesky | solution.py:99
  86.0 11.7 %cholesky.189 = f32[128,128]{1,0:T(8,128)S(1)} custom-call(f32[128,128]{1,0:T(8,128)S(1)} %convolution_subtract_fusion.10), custom_call_target="Cholesky" | custom-call | tf_op jit(solution)/shard_map/jit(cholesky)/cholesky | solution.py:99
  100.5 4.1 while.12
  104.6 20.1 %custom-call.25 = f32[2,128,128]{1,2,0:T(8,128)S(1)} custom-call(f32[2,128,128]{2,1,0:T(8,128)S(1)} %get-tuple-element.45), custom_call_target="InvertDiagBlocksLowerTriangular" | custom-call | tf_op jit(solution)/shard_map/jit(_cho_solve)/triangular_solve | solution.py:102
  135.8 8.5 %collective-permute-done.8 = f32[32,2832]{1,0:T(8,128)S(1)} collective-permute-done((f32[32,2832]{1,0:T(8,128)}, f32[32,2832]{1,0:T(8,128)S(1)}, u32[]{:S(2)}, u32[]{:S(2)}) %collective-permute-start.8) | collective-permute-done | bytes 362528 | tf_op jit(solution)/shard_map/ppermute | solution.py:17
  150.1 4.0 collective-permute-done.9
  159.6 4.0 collective-permute-done.10
  169.8 6.1 %collective-permute-done.11 = f32[32,2832]{1,0:T(8,128)S(1)} collective-permute-done((f32[32,2832]{1,0:T(8,128)S(1)}, f32[32,2832]{1,0:T(8,128)S(1)}, u32[]{:S(2)}, u32[]{:S(2)}) %collective-permute-start.11) | collective-permute-done | bytes 362528 | tf_op jit(solution)/shard_map/ppermute | solution.py:17
  181.4 11.3 %collective-permute-done.12 = f32[64,2832]{1,0:T(8,128)S(1)} collective-permute-done((f32[64,2832]{1,0:T(8,128)}, f32[64,2832]{1,0:T(8,128)S(1)}, u32[]{:S(2)}, u32[]{:S(2)}) %collective-permute-start.12) | collective-permute-done | bytes 725024 | tf_op jit(solution)/shard_map/ppermute | solution.py:89
  193.6 11.2 %collective-permute-done.13 = f32[64,2832]{1,0:T(8,128)} collective-permute-done((f32[64,2832]{1,0:T(8,128)S(1)}, f32[64,2832]{1,0:T(8,128)}, u32[]{:S(2)}, u32[]{:S(2)}) %collective-permute-start.13) | collective-permute-done | bytes 725024 | tf_op jit(solution)/shard_map/ppermute | solution.py:89
  210.1 6.2 %collective-permute-done.14 = f32[64,2832]{1,0:T(8,128)} collective-permute-done((f32[64,2832]{1,0:T(8,128)}, f32[64,2832]{1,0:T(8,128)}, u32[]{:S(2)}, u32[]{:S(2)}) %collective-permute-start.14) | collective-permute-done | bytes 725024 | tf_op jit(solution)/shard_map/ppermute | solution.py:89
  219.0 8.9 %concatenate.159 = f32[512,2832]{0,1:T(8,128)} concatenate(f32[64,2832]{0,1:T(8,128)} %copy.190, f32[64,2832]{0,1:T(8,128)} %copy.191, f32[64,2832]{0,1:T(8,128)S(1)} %copy.192, f32[64,2832]{0,1:T(8,128)S(1)} %maximum_select_fusion.4, f32[64,2832]{0,1:T(8,128)} %copy.190, f32[64,2832]{0,1:T(8,128)} %copy.191, f32[64,2832]{0,1:T(8,128)S(1)} %copy.192, ...), dimensions={0} | concatenate | bytes 11599872 | tf_op jit(solution)/shard_map/jit(_roll_dynamic)/concatenate | solution.py:90
  230.4 11.7 %cholesky.206 = f32[128,128]{1,0:T(8,128)S(1)} custom-call(f32[128,128]{1,0:T(8,128)S(1)} %cholesky.273), custom_call_target="Cholesky" | custom-call | tf_op jit(solution)/shard_map/jit(cholesky)/cholesky | solution.py:99
  242.2 9.8 %custom-call.26 = f32[1,128,128]{1,2,0:T(8,128)S(1)} custom-call(f32[1,128,128]{2,1,0:T(8,128)S(1)} %get-tuple-element.125), custom_call_target="InvertDiagBlocksLowerTriangular" | custom-call | tf_op jit(solution)/shard_map/jit(cholesky)/cholesky | solution.py:99
  252.5 11.7 %cholesky.223 = f32[128,128]{1,0:T(8,128)S(1)} custom-call(f32[128,128]{1,0:T(8,128)S(1)} %convolution_subtract_fusion.9), custom_call_target="Cholesky" | custom-call | tf_op jit(solution)/shard_map/jit(cholesky)/cholesky | solution.py:99
  266.9 4.1 while.13
  271.0 20.1 %custom-call.27 = f32[2,128,128]{1,2,0:T(8,128)S(1)} custom-call(f32[2,128,128]{2,1,0:T(8,128)S(1)} %get-tuple-element.46), custom_call_target="InvertDiagBlocksLowerTriangular" | custom-call | tf_op jit(solution)/shard_map/jit(_cho_solve)/triangular_solve | solution.py:102
  294.0 4.6 convolution_subtract_fusion
  306.1 12.8 %collective-permute-done.15 = f32[32,4880]{1,0:T(8,128)S(1)} collective-permute-done((f32[32,4880]{1,0:T(8,128)}, f32[32,4880]{1,0:T(8,128)S(1)}, u32[]{:S(2)}, u32[]{:S(2)}) %collective-permute-start.15) | collective-permute-done | bytes 624672 | tf_op jit(solution)/shard_map/ppermute | solution.py:17
  321.1 3.9 select_add_fusion.2
  331.8 5.8 collective-permute-done.16
  351.9 5.4 collective-permute-done.17
  359.4 3.9 select_add_fusion
  366.6 6.5 %collective-permute-done.18 = f32[8,4880]{1,0:T(8,128)S(1)} collective-permute-done((f32[8,4880]{1,0:T(8,128)S(1)}, f32[8,4880]{1,0:T(8,128)S(1)}, u32[]{:S(2)}, u32[]{:S(2)}) %collective-permute-start.18) | collective-permute-done | bytes 156192 | tf_op jit(solution)/shard_map/ppermute | solution.py:17
  374.8 5.4 collective-permute-done.19
  389.7 9.8 %collective-permute-done.20 = f32[32,4880]{1,0:T(8,128)} collective-permute-done((f32[32,4880]{1,0:T(8,128)}, f32[32,4880]{1,0:T(8,128)}, u32[]{:S(2)}, u32[]{:S(2)}) %collective-permute-start.20) | collective-permute-done | bytes 624672 | tf_op jit(solution)/shard_map/ppermute | solution.py:17
  402.8 5.3 maximum_select_fusion.1
  410.1 17.0 %collective-permute-done.21 = f32[64,4880]{1,0:T(8,128)} collective-permute-done((f32[64,4880]{1,0:T(8,128)}, f32[64,4880]{1,0:T(8,128)}, u32[]{:S(2)}, u32[]{:S(2)}) %collective-permute-start.21) | collective-permute-done | bytes 1249312 | tf_op jit(solution)/shard_map/ppermute | solution.py:89
  427.4 17.7 %all-gather = f32[1,16,1024]{2,1,0:T(8,128)S(1)} all-gather(f32[1,16,256]{2,1,0:T(8,128)S(1)} %copy-done.32), channel_id=2, replica_groups=mesh['leaf'=8,'blk'=4] {'blk'}, dimensions={2}, use_global_device_ids=true | all-gather | bytes 81920 | tf_op jit(solution)/shard_map/all_gather | solution.py:117
  450.9 3.9 collective-permute-done.1
  456.2 11.3 %collective-permute-done.2 = f32[16,4,1024]{2,0,1:T(8,128)S(1)} collective-permute-done((f32[16,4,1024]{2,0,1:T(8,128)S(1)}, f32[16,4,1024]{2,0,1:T(8,128)S(1)}, u32[]{:S(2)}, u32[]{:S(2)}) %collective-permute-start.2) | collective-permute-done | bytes 262176 | tf_op jit(solution)/shard_map/ppermute | solution.py:17
  479.3 15.1 %concatenate.170 = f32[512,4880]{0,1:T(8,128)} concatenate(f32[64,4880]{0,1:T(8,128)} %copy.213, f32[64,4880]{0,1:T(8,128)} %copy.214, f32[64,4880]{0,1:T(8,128)} %copy.215, f32[64,4880]{0,1:T(8,128)S(1)} %maximum_select_fusion.1, f32[64,4880]{0,1:T(8,128)} %copy.213, f32[64,4880]{0,1:T(8,128)} %copy.214, f32[64,4880]{0,1:T(8,128)} %copy.215, f32[64,4880]{0,1:T(8,128)S(1)} %maximum_select_fusion.1), dimensions={0} | concatenate | bytes 19988480 | tf_op jit(solution)/shard_map/jit(_roll_dynamic)/concatenate | solution.py:90
  496.8 11.7 %cholesky.240 = f32[128,128]{1,0:T(8,128)S(1)} custom-call(f32[128,128]{1,0:T(8,128)S(1)} %cholesky.276), custom_call_target="Cholesky" | custom-call | tf_op jit(solution)/shard_map/jit(cholesky)/cholesky | solution.py:99
  508.6 9.8 %custom-call.28 = f32[1,128,128]{1,2,0:T(8,128)S(1)} custom-call(f32[1,128,128]{2,1,0:T(8,128)S(1)} %get-tuple-element.121), custom_call_target="InvertDiagBlocksLowerTriangular" | custom-call | tf_op jit(solution)/shard_map/jit(cholesky)/cholesky | solution.py:99
  518.9 11.7 %cholesky.257 = f32[128,128]{1,0:T(8,128)S(1)} custom-call(f32[128,128]{1,0:T(8,128)S(1)} %convolution_subtract_fusion.8), custom_call_target="Cholesky" | custom-call | tf_op jit(solution)/shard_map/jit(cholesky)/cholesky | solution.py:99
  533.3 4.0 while.14
  537.3 19.9 %custom-call.29 = f32[2,128,128]{1,2,0:T(8,128)S(1)} custom-call(f32[2,128,128]{2,1,0:T(8,128)S(1)} %get-tuple-element.47), custom_call_target="InvertDiagBlocksLowerTriangular" | custom-call | tf_op jit(solution)/shard_map/jit(_cho_solve)/triangular_solve | solution.py:102
  557.2 6.1 %fusion.22 = f32[256,16]{0,1:T(8,128)S(1)} fusion(f32[512,4880]{0,1:T(8,128)} %concatenate.170, s32[]{:T(128)S(6)} %select_n.365, s32[]{:T(128)S(6)} %add.176, f32[16,256]{1,0:T(8,128)S(1)} %copy-done.26, f32[16,256]{1,0:T(8,128)S(1)} %copy-done.25, f32[16,4096]{1,0:T(8,128)S(1)} %bitcast.210, s32[]{:T(128)S(6)} %add.181), kind=kOutput, calls=%fused_computation.59 | convolution fusion | flops 226643968 | bytes 5048320 | tf_op jit(solution)/shard_map/dot_general | solution.py:142
  564.6 3.9 fusion.19
  575.9 9.4 %fusion.2 = f32[256,4608]{0,1:T(8,128)} fusion(f32[512,4880]{0,1:T(8,128)} %concatenate.170, s32[]{:T(128)S(6)} %select_n.365, s32[]{:T(128)S(6)} %add.176, f32[128,256]{1,0:T(8,128)S(1)} %fusion.65, f32[128,256]{1,0:T(8,128)S(1)} %fusion.62), kind=kOutput, calls=%fused_computation.8 | convolution fusion | flops 3623944192 | bytes 9699336 | tf_op jit(solution)/shard_map/dot_general | solution.py:112
  587.7 3.8 fusion.26
  (313 shorter events, 175.8 us)
Async XLA Ops:
  4.0 9.0 %collective-permute-start.3 = (f32[32,1808]{1,0:T(8,128)S(1)}, f32[32,1808]{1,0:T(8,128)S(1)}, u32[]{:S(2)}, u32[]{:S(2)}) collective-permute-start(f32[32,1808]{1,0:T(8,128)S(1)} %copy.165), channel_id=1, source_target_pairs={{0,4},{4,0},{8,12},{12,8},{16,20},{20,16},{24,28},{28,24},{1,5},{5... | collective-permute-start | bytes 694280 | tf_op jit(solution)/shard_map/ppermute | solution.py:17
  16.0 7.2 %collective-permute-start.4 = (f32[32,1808]{1,0:T(8,128)S(1)}, f32[32,1808]{1,0:T(8,128)S(1)}, u32[]{:S(2)}, u32[]{:S(2)}) collective-permute-start(f32[32,1808]{1,0:T(8,128)S(1)} %copy.167), channel_id=1, source_target_pairs={{0,4},{4,0},{8,12},{12,8},{16,20},{20,16},{24,28},{28,24},{1,5},{5... | collective-permute-start | bytes 694280 | tf_op jit(solution)/shard_map/ppermute | solution.py:17
  26.8 8.3 %collective-permute-start.5 = (f32[64,1808]{1,0:T(8,128)S(1)}, f32[64,1808]{1,0:T(8,128)S(1)}, u32[]{:S(2)}, u32[]{:S(2)}) collective-permute-start(f32[64,1808]{1,0:T(8,128)S(1)} %copy.170), channel_id=1, source_target_pairs={{0,1},{1,2},{2,3},{3,0},{4,5},{5,6},{6,7},{7,4},{8,9},{9,10},{10,1... | collective-permute-start | bytes 1388552 | tf_op jit(solution)/shard_map/ppermute | solution.py:89
  35.9 8.4 %collective-permute-start.6 = (f32[64,1808]{1,0:T(8,128)S(1)}, f32[64,1808]{1,0:T(8,128)}, u32[]{:S(2)}, u32[]{:S(2)}) collective-permute-start(f32[64,1808]{1,0:T(8,128)S(1)} %collective-permute-done.5), channel_id=1, source_target_pairs={{0,1},{1,2},{2,3},{3,0},{4,5},{5,6},{6,7},{7,4},{8,9},{9,10},{10,1... | collective-permute-start | bytes 1388552 | tf_op jit(solution)/shard_map/ppermute | solution.py:89
  44.3 8.8 %collective-permute-start.7 = (f32[64,1808]{1,0:T(8,128)}, f32[64,1808]{1,0:T(8,128)}, u32[]{:S(2)}, u32[]{:S(2)}) collective-permute-start(f32[64,1808]{1,0:T(8,128)} %collective-permute-done.6), channel_id=1, source_target_pairs={{0,1},{1,2},{2,3},{3,0},{4,5},{5,6},{6,7},{7,4},{8,9},{9,10},{10,1... | collective-permute-start | bytes 1388552 | tf_op jit(solution)/shard_map/ppermute | solution.py:89
  63.9 62.7 %copy-start.30 = (f32[1,16,256]{2,1,0:T(8,128)S(1)}, f32[1,16,256]{2,1,0:T(8,128)}, u32[]{:S(2)}) copy-start(f32[1,16,256]{2,1,0:T(8,128)} %param.9) | copy-start | bytes 49156
  86.0 42.3 %copy-start.14 = (f32[256,512]{0,1:T(8,128)S(1)}, f32[256,512]{0,1:T(8,128)}, u32[]{:S(2)}) copy-start(f32[256,512]{0,1:T(8,128)} %slice.419) | copy-start | bytes 1572868
  86.0 42.3 %copy-start.23 = (f32[256,256]{0,1:T(8,128)S(1)}, f32[256,256]{0,1:T(8,128)}, u32[]{:S(2)}) copy-start(f32[256,256]{0,1:T(8,128)} %get-tuple-element.100) | copy-start | bytes 786436
  86.0 42.3 %copy-start.24 = (f32[256,256]{0,1:T(8,128)S(1)}, f32[256,256]{0,1:T(8,128)}, u32[]{:S(2)}) copy-start(f32[256,256]{0,1:T(8,128)} %get-tuple-element.101) | copy-start | bytes 786436
  124.8 6.7 %copy-start.8 = (f32[2,128,128]{1,2,0:T(8,128)}, f32[2,128,128]{1,2,0:T(8,128)S(1)}, u32[]{:S(2)}) copy-start(f32[2,128,128]{1,2,0:T(8,128)S(1)} %custom-call.25) | copy-start | bytes 393220
  127.5 4.5 copy-start.27
  134.3 10.0 %collective-permute-start.8 = (f32[32,2832]{1,0:T(8,128)}, f32[32,2832]{1,0:T(8,128)S(1)}, u32[]{:S(2)}, u32[]{:S(2)}) collective-permute-start(f32[32,2832]{1,0:T(8,128)} %copy.179), channel_id=1, source_target_pairs={{0,4},{4,0},{8,12},{12,8},{16,20},{20,16},{24,28},{28,24},{1,5},{5... | collective-permute-start | bytes 1087496 | tf_op jit(solution)/shard_map/ppermute | solution.py:17
  148.5 5.6 collective-permute-start.9
  157.9 5.6 collective-permute-start.10
  168.2 7.7 %collective-permute-start.11 = (f32[32,2832]{1,0:T(8,128)S(1)}, f32[32,2832]{1,0:T(8,128)S(1)}, u32[]{:S(2)}, u32[]{:S(2)}) collective-permute-start(f32[32,2832]{1,0:T(8,128)S(1)} %copy.186), channel_id=1, source_target_pairs={{0,4},{4,0},{8,12},{12,8},{16,20},{20,16},{24,28},{28,24},{1,5},{5... | collective-permute-start | bytes 1087496 | tf_op jit(solution)/shard_map/ppermute | solution.py:17
  180.1 24.9 %copy-start.7 = (f32[256,1536]{0,1:T(8,128)S(1)}, f32[256,1536]{0,1:T(8,128)}, u32[]{:S(2)}) copy-start(f32[256,1536]{0,1:T(8,128)} %copy-done.6) | copy-start | bytes 4718596
  181.4 11.3 %collective-permute-start.12 = (f32[64,2832]{1,0:T(8,128)}, f32[64,2832]{1,0:T(8,128)S(1)}, u32[]{:S(2)}, u32[]{:S(2)}) collective-permute-start(f32[64,2832]{1,0:T(8,128)} %copy.189), channel_id=1, source_target_pairs={{0,1},{1,2},{2,3},{3,0},{4,5},{5,6},{6,7},{7,4},{8,9},{9,10},{10,1... | collective-permute-start | bytes 2174984 | tf_op jit(solution)/shard_map/ppermute | solution.py:89
  193.6 11.2 %collective-permute-start.13 = (f32[64,2832]{1,0:T(8,128)S(1)}, f32[64,2832]{1,0:T(8,128)}, u32[]{:S(2)}, u32[]{:S(2)}) collective-permute-start(f32[64,2832]{1,0:T(8,128)S(1)} %collective-permute-done.12), channel_id=1, source_target_pairs={{0,1},{1,2},{2,3},{3,0},{4,5},{5,6},{6,7},{7,4},{8,9},{9,10},{10,1... | collective-permute-start | bytes 2174984 | tf_op jit(solution)/shard_map/ppermute | solution.py:89
  204.8 11.5 %collective-permute-start.14 = (f32[64,2832]{1,0:T(8,128)}, f32[64,2832]{1,0:T(8,128)}, u32[]{:S(2)}, u32[]{:S(2)}) collective-permute-start(f32[64,2832]{1,0:T(8,128)} %collective-permute-done.13), channel_id=1, source_target_pairs={{0,1},{1,2},{2,3},{3,0},{4,5},{5,6},{6,7},{7,4},{8,9},{9,10},{10,1... | collective-permute-start | bytes 2174984 | tf_op jit(solution)/shard_map/ppermute | solution.py:89
  230.4 62.5 %copy-start.28 = (f32[16,256]{1,0:T(8,128)S(1)}, f32[16,256]{1,0:T(8,128)}, u32[]{:S(2)}) copy-start(f32[16,256]{1,0:T(8,128)} %copy-done.27) | copy-start | bytes 49156
  266.9 27.1 %slice-start.1 = ((f32[256,1536]{0,1:T(8,128)}), f32[256,1024]{0,1:T(8,128)S(1)}, s32[]{:S(2)}) async-start(f32[256,1536]{0,1:T(8,128)} %copy-done.6), calls=%async_computation.1 | async-start | bytes 2097152 | tf_op jit(solution)/shard_map/slice | solution.py:110
  266.9 27.1 %copy-start.19 = (f32[256,256]{0,1:T(8,128)S(1)}, f32[256,256]{0,1:T(8,128)}, u32[]{:S(2)}) copy-start(f32[256,256]{0,1:T(8,128)} %copy-done.18) | copy-start | bytes 786436
  291.1 7.5 %copy-start.10 = (f32[2,128,128]{1,2,0:T(8,128)}, f32[2,128,128]{1,2,0:T(8,128)S(1)}, u32[]{:S(2)}) copy-start(f32[2,128,128]{1,2,0:T(8,128)S(1)} %custom-call.27) | copy-start | bytes 393220
  293.9 6.4 %copy-start.31 = (f32[16,256]{1,0:T(8,128)}, f32[16,256]{1,0:T(8,128)S(1)}, u32[]{:S(2)}) copy-start(f32[16,256]{1,0:T(8,128)S(1)} %convolution_subtract_fusion.11) | copy-start | bytes 49156
  304.6 14.3 %collective-permute-start.15 = (f32[32,4880]{1,0:T(8,128)}, f32[32,4880]{1,0:T(8,128)S(1)}, u32[]{:S(2)}, u32[]{:S(2)}) collective-permute-start(f32[32,4880]{1,0:T(8,128)} %copy.198), channel_id=1, source_target_pairs={{0,4},{4,0},{8,12},{12,8},{16,20},{20,16},{24,28},{28,24},{1,5},{5... | collective-permute-start | bytes 1873928 | tf_op jit(solution)/shard_map/ppermute | solution.py:17
  330.3 7.3 %collective-permute-start.16 = (f32[16,4880]{1,0:T(8,128)}, f32[16,4880]{1,0:T(8,128)}, u32[]{:S(2)}, u32[]{:S(2)}) collective-permute-start(f32[16,4880]{1,0:T(8,128)} %copy.200), channel_id=1, source_target_pairs={{0,8},{8,0},{4,12},{12,4},{16,24},{24,16},{20,28},{28,20},{1,9},{9... | collective-permute-start | bytes 936968 | tf_op jit(solution)/shard_map/ppermute | solution.py:17
  346.8 12.6 %copy-start.2 = (f32[16,4880]{0,1:T(8,128)S(1)}, f32[16,4880]{0,1:T(8,128)}, u32[]{:S(2)}) copy-start(f32[16,4880]{0,1:T(8,128)} %copy-done.1) | copy-start | bytes 936964
  349.3 7.9 %collective-permute-start.17 = (f32[8,4880]{1,0:T(8,128)S(1)}, f32[8,4880]{1,0:T(8,128)S(1)}, u32[]{:S(2)}, u32[]{:S(2)}) collective-permute-start(f32[8,4880]{1,0:T(8,128)S(1)} %copy.202), channel_id=1, source_target_pairs={{0,16},{16,0},{4,20},{20,4},{8,24},{24,8},{12,28},{28,12},{1,17},{... | collective-permute-start | bytes 468488 | tf_op jit(solution)/shard_map/ppermute | solution.py:17
  365.7 7.4 %collective-permute-start.18 = (f32[8,4880]{1,0:T(8,128)S(1)}, f32[8,4880]{1,0:T(8,128)S(1)}, u32[]{:S(2)}, u32[]{:S(2)}) collective-permute-start(f32[8,4880]{1,0:T(8,128)S(1)} %copy.204), channel_id=1, source_target_pairs={{0,16},{16,0},{4,20},{20,4},{8,24},{24,8},{12,28},{28,12},{1,17},{... | collective-permute-start | bytes 468488 | tf_op jit(solution)/shard_map/ppermute | solution.py:17
  373.1 7.1 %collective-permute-start.19 = (f32[16,4880]{1,0:T(8,128)S(1)}, f32[16,4880]{1,0:T(8,128)S(1)}, u32[]{:S(2)}, u32[]{:S(2)}) collective-permute-start(f32[16,4880]{1,0:T(8,128)S(1)} %maximum_select_fusion.7), channel_id=1, source_target_pairs={{0,8},{8,0},{4,12},{12,4},{16,24},{24,16},{20,28},{28,20},{1,9},{9... | collective-permute-start | bytes 936968 | tf_op jit(solution)/shard_map/ppermute | solution.py:17
  386.7 12.9 %copy-start.3 = (f32[32,4880]{0,1:T(8,128)}, f32[32,4880]{0,1:T(8,128)S(1)}, u32[]{:S(2)}) copy-start(f32[32,4880]{0,1:T(8,128)S(1)} %broadcast_select_fusion) | copy-start | bytes 1873924
  388.3 11.2 %collective-permute-start.20 = (f32[32,4880]{1,0:T(8,128)}, f32[32,4880]{1,0:T(8,128)}, u32[]{:S(2)}, u32[]{:S(2)}) collective-permute-start(f32[32,4880]{1,0:T(8,128)} %copy.209), channel_id=1, source_target_pairs={{0,4},{4,0},{8,12},{12,8},{16,20},{20,16},{24,28},{28,24},{1,5},{5... | collective-permute-start | bytes 1873928 | tf_op jit(solution)/shard_map/ppermute | solution.py:17
  408.1 19.3 %copy-start.32 = (f32[1,16,256]{2,1,0:T(8,128)S(1)}, f32[1,16,256]{2,1,0:T(8,128)}, u32[]{:S(2)}) copy-start(f32[1,16,256]{2,1,0:T(8,128)} %param.10) | copy-start | bytes 49156
  410.1 17.0 %collective-permute-start.21 = (f32[64,4880]{1,0:T(8,128)}, f32[64,4880]{1,0:T(8,128)}, u32[]{:S(2)}, u32[]{:S(2)}) collective-permute-start(f32[64,4880]{1,0:T(8,128)} %copy.212), channel_id=1, source_target_pairs={{0,1},{1,2},{2,3},{3,0},{4,5},{5,6},{6,7},{7,4},{8,9},{9,10},{10,1... | collective-permute-start | bytes 3747848 | tf_op jit(solution)/shard_map/ppermute | solution.py:89
  427.1 29.1 %collective-permute-start.22 = (f32[64,4880]{1,0:T(8,128)}, f32[64,4880]{1,0:T(8,128)}, u32[]{:S(2)}, u32[]{:S(2)}) collective-permute-start(f32[64,4880]{1,0:T(8,128)} %collective-permute-done.21), channel_id=1, source_target_pairs={{0,1},{1,2},{2,3},{3,0},{4,5},{5,6},{6,7},{7,4},{8,9},{9,10},{10,1... | collective-permute-start | bytes 3747848 | tf_op jit(solution)/shard_map/ppermute | solution.py:89
  445.4 4.3 collective-permute-start
  449.8 5.0 collective-permute-start.1
  454.8 12.7 %collective-permute-start.2 = (f32[16,4,1024]{2,0,1:T(8,128)S(1)}, f32[16,4,1024]{2,0,1:T(8,128)S(1)}, u32[]{:S(2)}, u32[]{:S(2)}) collective-permute-start(f32[16,4,1024]{2,0,1:T(8,128)S(1)} %maximum_select_fusion.8), channel_id=1, source_target_pairs={{0,16},{16,0},{4,20},{20,4},{8,24},{24,8},{12,28},{28,12},{1,17},{... | collective-permute-start | bytes 786440 | tf_op jit(solution)/shard_map/ppermute | solution.py:17
  456.2 20.2 %collective-permute-start.23 = (f32[64,4880]{1,0:T(8,128)}, f32[64,4880]{1,0:T(8,128)}, u32[]{:S(2)}, u32[]{:S(2)}) collective-permute-start(f32[64,4880]{1,0:T(8,128)} %collective-permute-done.22), channel_id=1, source_target_pairs={{0,1},{1,2},{2,3},{3,0},{4,5},{5,6},{6,7},{7,4},{8,9},{9,10},{10,1... | collective-permute-start | bytes 3747848 | tf_op jit(solution)/shard_map/ppermute | solution.py:89
  494.4 62.8 %copy-start.25 = (f32[16,256]{1,0:T(8,128)S(1)}, f32[16,256]{1,0:T(8,128)}, u32[]{:S(2)}) copy-start(f32[16,256]{1,0:T(8,128)} %get-tuple-element.106) | copy-start | bytes 49156
  494.4 62.8 %copy-start.26 = (f32[16,256]{1,0:T(8,128)S(1)}, f32[16,256]{1,0:T(8,128)}, u32[]{:S(2)}) copy-start(f32[16,256]{1,0:T(8,128)} %get-tuple-element.107) | copy-start | bytes 49156
  557.2 7.3 %copy-start.15 = (f32[16,2048]{1,0:T(8,128)S(1)}, f32[16,2048]{1,0:T(8,128)}, u32[]{:S(2)}) copy-start(f32[16,2048]{1,0:T(8,128)} %get-tuple-element.108) | copy-start | bytes 393220
  557.2 7.3 %copy-start.16 = (f32[16,2048]{1,0:T(8,128)S(1)}, f32[16,2048]{1,0:T(8,128)}, u32[]{:S(2)}) copy-start(f32[16,2048]{1,0:T(8,128)} %get-tuple-element.109) | copy-start | bytes 393220
  563.3 5.2 copy-start.11
  564.5 8.0 %copy-start.12 = (f32[256,256]{1,0:T(8,128)S(1)}, f32[256,256]{1,0:T(8,128)}, u32[]{:S(2)}) copy-start(f32[256,256]{1,0:T(8,128)} %get-tuple-element.82) | copy-start | bytes 786436
  575.9 9.4 %copy-start.9 = (f32[2,128,128]{1,2,0:T(8,128)S(1)}, f32[2,128,128]{1,2,0:T(8,128)}, u32[]{:S(2)}) copy-start(f32[2,128,128]{1,2,0:T(8,128)} %copy-done.8) | copy-start | bytes 393220
  585.3 2.3 copy-start.21
  585.3 2.3 copy-start.22
  (11 other events, 15.2 us)
